TPU v7x, 256 devices: a whole 4x4x8 slice. The times are simulated.
256 devices in a mesh: tok: 64 (over z_hi, x, y), head: 4 (over z_lo, core).
Axes of the slice: x: 4, y: 4, z: 8 (z_hi: 4, z_lo: 2; z = z_hi * 2 + z_lo), core: 2. Of those that a mesh axis runs over, the one named last changes fastest.
Arguments:
- queries: bfloat16 [16384, 2560], P('tok', 'head'), may hold values from -140 to 140
- keys: bfloat16 [2048, 2560], P('tok', 'head'), may hold values from -6 to 6
- values: bfloat16 [2048, 2560], P('tok', 'head'), may hold values from -6 to 6
- query_tan: bfloat16 [16384, 2560], P('tok', 'head'), may hold values from -6 to 6
- key_tan: bfloat16 [2048, 2560], P('tok', 'head'), may hold values from -6 to 6
- value_tan: bfloat16 [2048, 2560], P('tok', 'head'), may hold values from -6 to 6
- out_weight: bfloat16 [2560, 5120], P('head'), may hold values from -0.3125 to 0.3125
Outputs:
- output: bfloat16 [16384, 5120], P('tok', 'head')
- output_tan: bfloat16 [16384, 5120], P('tok', 'head')
All inputs are finite; a program needn't handle non-finite values.
Results may differ from a plain program's by a relative error of at most 0.012.
Values may be sent and summed in bfloat16 or wider, within the bound.
No kernel may reach another device: no remote copies, remote signals or barrier semaphores. Data moves between devices by JAX's collectives and lax.ppermute only.
A program may use at most 128 MiB of HBM per device.

v0:
```python
import jax
import jax.numpy as jnp
from jax import lax
from jax.sharding import PartitionSpec as P

HD = 128


def split_rows(array, head_count):
    return array.reshape(array.shape[0], head_count, HD)


def score_pair(query_heads, query_dir_heads, key_piece, key_dir_piece, head_count, score_scale):
    key_heads = split_rows(key_piece, head_count)
    key_dir_heads = split_rows(key_dir_piece, head_count)
    scores = (
        jnp.einsum("thd,rhd->htr", query_heads, key_heads, preferred_element_type=jnp.float32)
        * score_scale
    )
    tangent = (
        jnp.einsum("thd,rhd->htr", query_dir_heads, key_heads, preferred_element_type=jnp.float32)
        + jnp.einsum("thd,rhd->htr", query_heads, key_dir_heads, preferred_element_type=jnp.float32)
    ) * score_scale
    return (scores, tangent)


def apply_weights(weights, value_heads):
    return jnp.einsum("htr,rhd->htd", weights, value_heads, preferred_element_type=jnp.float32)


def join_heads(array, rows_here, head_count):
    return array.transpose(1, 0, 2).reshape(rows_here, head_count * HD).astype(jnp.bfloat16)


def shards(queries, keys, values, query_tan, key_tan, value_tan, out_weight):
    rows_here = queries.shape[0]
    head_count = queries.shape[1] // HD
    score_scale = HD ** (-0.5)
    query_heads = split_rows(queries, head_count)
    query_dir_heads = split_rows(query_tan, head_count)
    lowest = jnp.full((head_count, rows_here), -1e30, jnp.float32)
    stacked_all = jnp.stack((keys, values, key_tan, value_tan))
    stacked_pair = jnp.stack((keys, values))
    pieces = lax.all_gather(stacked_pair, "tok", axis=1, tiled=True)
    key_heads = split_rows(pieces[0], head_count)
    value_heads = split_rows(pieces[1], head_count)
    scores = (
        jnp.einsum("thd,rhd->htr", query_heads, key_heads, preferred_element_type=jnp.float32)
        * score_scale
    )
    peak_new = jnp.maximum(lowest, jnp.max(scores, axis=2))
    exponent = jnp.exp(scores - peak_new[:, :, None])
    row_total = jnp.sum(exponent, axis=2)
    numerator = apply_weights(exponent.astype(jnp.bfloat16), value_heads)
    peak, row_total, numerator = (peak_new, row_total, numerator)
    attended = numerator / row_total[:, :, None]
    pieces = lax.all_gather(stacked_all, "tok", axis=1, tiled=True)
    scores, tangent = score_pair(
        query_heads, query_dir_heads, pieces[0], pieces[2], head_count, score_scale
    )
    value_heads = split_rows(pieces[1], head_count)
    value_dir_heads = split_rows(pieces[3], head_count)
    exponent = jnp.exp(scores - peak[:, :, None])
    weighted = exponent * tangent
    row_total_tan = jnp.sum(weighted, axis=2)
    numerator_tan = apply_weights(weighted.astype(jnp.bfloat16), value_heads) + apply_weights(
        exponent.astype(jnp.bfloat16), value_dir_heads
    )
    row_total_tan, numerator_tan = (row_total_tan, numerator_tan)
    attended_tan = (numerator_tan - attended * row_total_tan[:, :, None]) / row_total[:, :, None]
    partial_value = jnp.dot(
        join_heads(attended, rows_here, head_count), out_weight, preferred_element_type=jnp.float32
    )
    partial_tan = jnp.dot(
        join_heads(attended_tan, rows_here, head_count),
        out_weight,
        preferred_element_type=jnp.float32,
    )
    output, output_tan = (
        lax.psum_scatter(
            partial_value.astype(jnp.bfloat16), "head", scatter_dimension=1, tiled=True
        ).astype(jnp.float32),
        lax.psum_scatter(
            partial_tan.astype(jnp.bfloat16), "head", scatter_dimension=1, tiled=True
        ).astype(jnp.float32),
    )
    return (output.astype(jnp.bfloat16), output_tan.astype(jnp.bfloat16))


def solution(mesh):
    in_specs = (
        P("tok", "head"),
        P("tok", "head"),
        P("tok", "head"),
        P("tok", "head"),
        P("tok", "head"),
        P("tok", "head"),
        P("head", None),
    )
    out_specs = (P("tok", "head"), P("tok", "head"))
    return jax.shard_map(shards, mesh=mesh, in_specs=in_specs, out_specs=out_specs, check_vma=False)
```

profile of v0, /device:TPU:1, one launch (start us, length us, event | category | flops | bytes accessed | tf_op | source)
XLA Modules:
  0.0 385.8 jit_solution(15764494412756072858)
XLA Ops:
  8.8 0.9 pad_maximum_fusion
  10.5 1.1 copy.36
  11.6 1.1 copy.45
  12.8 97.5 %all-gather.3.cloned.1.call-done = bf16[2,2048,640]{2,0,1:T(2,128)(2,1)} async-done(((bf16[2,32,640]{2,0,1:T(2,128)(2,1)}), bf16[2,2048,640]{2,0,1:T(2,128)(2,1)}) %all-gather.3.cloned.1.call-update) | async-done | bytes 5242896 | tf_op jit(solution)/shard_map/all_gather | solution.py:44
  110.3 11.9 %fusion.38 = (bf16[1,2048,640]{2,0,1:T(2,128)(2,1)}, bf16[1,2048,640]{2,0,1:T(2,128)(2,1)}) fusion(bf16[2,2048,640]{2,0,1:T(2,128)(2,1)} %all-gather.3.cloned.1.call-done), kind=kLoop, calls=%fused_computation.32 | loop fusion | bytes 10485760 | tf_op jit(solution)/shard_map/slice | solution.py:45
  122.2 9.7 %copy.64 = bf16[1,2048,640]{1,2,0:T(8,128)(2,1)S(1)} copy(bf16[1,2048,640]{2,0,1:T(2,128)(2,1)} %get-tuple-element.6) | data formatting | bytes 5242880
  131.9 11.1 %copy.39 = bf16[1,2048,640]{1,2,0:T(8,128)(2,1)} copy(bf16[1,2048,640]{2,0,1:T(2,128)(2,1)} %get-tuple-element.7) | data formatting | bytes 5242880 | tf_op jit(solution)/shard_map/slice | solution.py:46
  143.0 1.6 bitcast_reduce_fusion.1
  144.7 1.7 fusion.2
  146.4 2.7 fusion.39
  149.1 3.7 convolution_convert_fusion.1
  153.1 86.9 %all-gather.5.cloned.1.call-done = bf16[4,2048,640]{2,0,1:T(4,128)(2,1)} async-done(((bf16[4,32,640]{2,0,1:T(4,128)(2,1)}), bf16[4,2048,640]{2,0,1:T(4,128)(2,1)}) %all-gather.5.cloned.1.call-update) | async-done | bytes 10485776 | tf_op jit(solution)/shard_map/all_gather | solution.py:57
  240.0 28.6 %fusion.37 = (bf16[1,2048,640]{2,0,1:T(2,128)(2,1)}, bf16[1,2048,640]{2,0,1:T(2,128)(2,1)}, bf16[1,2048,640]{2,0,1:T(2,128)(2,1)}, bf16[1,2048,640]{2,0,1:T(2,128)(2,1)}) fusion(bf16[4,2048,640]{2,0,1:T(4,128)(2,1)} %all-gather.5.cloned.1.call-done), kind=kLoop, calls=%fused_computation.31 | loop fusion | bytes 20971520 | tf_op jit(solution)/shard_map/slice | solution.py:62
  268.6 11.1 %copy.53 = bf16[1,2048,640]{1,2,0:T(8,128)(2,1)} copy(bf16[1,2048,640]{2,0,1:T(2,128)(2,1)} %get-tuple-element.2) | data formatting | bytes 5242880 | tf_op jit(solution)/shard_map/slice | solution.py:62
  279.7 9.7 %copy.65 = bf16[1,2048,640]{1,2,0:T(8,128)(2,1)S(1)} copy(bf16[1,2048,640]{2,0,1:T(2,128)(2,1)} %get-tuple-element.3) | data formatting | bytes 5242880
  289.4 11.1 %copy.51 = bf16[1,2048,640]{1,2,0:T(8,128)(2,1)} copy(bf16[1,2048,640]{2,0,1:T(2,128)(2,1)} %get-tuple-element.4) | data formatting | bytes 5242880 | tf_op jit(solution)/shard_map/slice | solution.py:61
  300.5 11.1 %copy.66 = bf16[1,2048,640]{1,2,0:T(8,128)(2,1)} copy(bf16[1,2048,640]{2,0,1:T(2,128)(2,1)} %get-tuple-element.5) | data formatting | bytes 5242880
  311.6 5.5 %fusion.42 = f32[5,2048,256]{2,1,0:T(8,128)} fusion(bf16[2048,5,128]{0,2,1:T(8,128)(2,1)S(1)} %bitcast.70, bf16[256,5,128]{0,2,1:T(8,128)(2,1)S(1)} %bitcast.76), kind=kOutput, calls=%fused_computation.36 | convolution fusion | flops 671088640 | bytes 13434880 | tf_op jit(solution)/shard_map/thd,rhd->htr/dot_general | solution.py:17
  317.2 5.5 %fusion.43 = f32[5,2048,256]{2,1,0:T(8,128)} fusion(bf16[2048,5,128]{0,2,1:T(8,128)(2,1)S(1)} %bitcast.71, bf16[256,5,128]{0,2,1:T(8,128)(2,1)S(1)} %bitcast.80), kind=kOutput, calls=%fused_computation.37 | convolution fusion | flops 671088640 | bytes 13434880 | tf_op jit(solution)/shard_map/thd,rhd->htr/dot_general | solution.py:21
  322.7 10.3 %bitcast_reduce_fusion = (f32[5,256]{1,0:T(8,128)S(1)}, bf16[5,2048,256]{2,1,0:T(8,128)(2,1)S(1)}) fusion(f32[5,2048,256]{2,1,0:T(8,128)} %fusion.43, bf16[2048,5,128]{0,2,1:T(8,128)(2,1)} %bitcast.73, bf16[256,5,128]{0,2,1:T(8,128)(2,1)S(1)} %bitcast.77, f32[5,256]{1,0:T(8,128)S(1)} %broadcast_maximum_fusion, f32[5,2048,256]{2,1,0:T(8,128)} %fusion.42), kind=kOutput, calls=%fused_computation | convolution fusion | flops 689437440 | bytes 29173760 | tf_op jit(solution)/shard_map/thd,rhd->htr/dot_general | solution.py:22
  333.0 0.8 fusion.40
  334.8 6.3 %fusion.31 = bf16[256,5,128]{0,2,1:T(8,128)(2,1)S(1)} fusion(f32[5,256,128]{1,2,0:T(8,128)S(1)} %fusion.40, bf16[2048,5,128]{0,2,1:T(8,128)(2,1)S(1)} %bitcast.78, f32[5,2048,256]{2,1,0:T(8,128)} %fusion.42, f32[5,256]{1,0:T(8,128)S(1)} %broadcast_maximum_fusion, f32[256,5,128]{0,2,1:T(8,128)S(1)} %copy-done.3, f32[256,5]{0,1:T(8,128)S(1)} %bitcast.91, ...), kind=kOutput, calls=%fused_computation.25 | convolution fusion | flops 679772160 | bytes 14760960 | tf_op jit(solution)/shard_map/htr,rhd->htd/dot_general | solution.py:28
  341.2 3.8 convolution_convert_fusion
  345.1 34.2 %reduce-scatter.5.cloned.1.call-done = bf16[256,1280]{1,0:T(8,128)(2,1)} async-done(((bf16[256,5120]{1,0:T(8,128)(2,1)}), bf16[256,1280]{1,0:T(8,128)(2,1)}) %reduce-scatter.5.cloned.1.call-update) | async-done | bytes 655376 | tf_op jit(solution)/shard_map/reduce_scatter | solution.py:83
  (31 shorter events, 3.7 us)
Async XLA Ops:
  7.2 103.1 %all-gather.3.cloned.1.call-start = ((), (), s32[]{:S(2)}) async-start(), calls=%async_computation.2 | async-start | bytes 5324800 | tf_op jit(solution)/shard_map/all_gather | solution.py:44
  8.7 231.3 %all-gather.5.cloned.1.call-start = ((), (), s32[]{:S(2)}) async-start(), calls=%async_computation.4 | async-start | bytes 10649600 | tf_op jit(solution)/shard_map/all_gather | solution.py:57
  10.5 334.6 %reduce-scatter.3.cloned.1.call-start = ((), (), s32[]{:S(2)}) async-start(), calls=%async_computation.3 | async-start | bytes 3276800 | tf_op jit(solution)/shard_map/reduce_scatter | solution.py:80
  144.6 1.7 copy-start.2
  144.6 4.5 %slice-start = ((s8[6553600]{0:T(1024)(128)(4,1)}), s8[4194304]{0:T(1024)(128)(4,1)S(1)}, s32[]{:S(2)}) async-start(s8[6553600]{0:T(1024)(128)(4,1)} %bitcast.66), calls=%async_computation.6 | async-start | bytes 8388608
  146.4 2.8 slice-start.1
  152.9 226.3 %reduce-scatter.5.cloned.1.call-start = ((), (), s32[]{:S(2)}) async-start(), calls=%async_computation.5 | async-start | bytes 3276800 | tf_op jit(solution)/shard_map/reduce_scatter | solution.py:83
  322.7 10.3 %copy-start = (bf16[1,2048,640]{1,2,0:T(8,128)(2,1)S(1)}, bf16[1,2048,640]{1,2,0:T(8,128)(2,1)}, u32[]{:S(2)}) copy-start(bf16[1,2048,640]{1,2,0:T(8,128)(2,1)} %copy.51) | copy-start | bytes 7864324
  333.0 1.7 copy-start.1
  333.0 1.9 copy-start.3
  333.0 8.2 %slice-start.2 = ((s8[6553600]{0:T(1024)(128)(4,1)}), s8[4194304]{0:T(1024)(128)(4,1)S(1)}, s32[]{:S(2)}) async-start(s8[6553600]{0:T(1024)(128)(4,1)} %bitcast.68), calls=%async_computation.8 | async-start | bytes 8388608
  334.8 6.3 %slice-start.3 = ((s8[6553600]{0:T(1024)(128)(4,1)}), s8[2359296]{0:T(1024)(128)(4,1)S(1)}, s32[]{:S(2)}) async-start(s8[6553600]{0:T(1024)(128)(4,1)} %bitcast.68), calls=%async_computation.9 | async-start | bytes 4718592
Sparse Core Ops, SparseCore 0:
  11.8 98.3 all-gather.2
  113.6 126.3 all-gather.4
  243.1 33.9 reduce-scatter.2
  345.2 34.0 reduce-scatter.4
where the time goes:
time: 387 us; the launch traced here: 386 us
  waiting for transfers between devices  219 us (57%)
  local copies, waits for them, and re-layouts  109 us (28%)
  matrix products  40.4 us (10%)
  between operations  13.9 us (4%)
    all_gather x1, waiting for transfers between devices, shards(): pieces = lax.all_gather(stacked_pair, 'tok', axis=1, tiled=True)  97.5 us
    all_gather x1, waiting for transfers between devices, shards(): pieces = lax.all_gather(stacked_all, 'tok', axis=1, tiled=True)  86.9 us
    slice x2, local copies, waits for them, and re-layouts, shards(): value_dir_heads = split_rows(pieces[3], head_count)  39.7 us
    reduce_scatter x1, waiting for transfers between devices, shards(): lax.psum_scatter(partial_tan.astype(jnp.bfloat16), 'head', scatter_dimens...  34.2 us
    unnamed x21, local copies, waits for them, and re-layouts  33.8 us
    slice x2, local copies, waits for them, and re-layouts, shards(): value_heads = split_rows(pieces[1], head_count)  22.3 us
    slice x1, local copies, waits for them, and re-layouts, shards(): key_heads = split_rows(pieces[0], head_count)  11.9 us
    dot_general x1, matrix products, score_pair(): jnp.einsum('thd,rhd->htr', query_heads, key_dir_heads, preferred_element_...  10.3 us
  transfers between devices with their start and end apart: 4, of which 3 were waited for; matrix products, arithmetic and copies ran while one was open for 39% of the time, Pallas kernels for 0%

commit v1 on v0

--- a/solution.py
+++ b/solution.py
@@ -4,6 +4,11 @@
 from jax.sharding import PartitionSpec as P
 
 HD = 128
+
+
+def slabs_rest(block_here, across):
+    small = lax.all_gather(block_here, axis_name=across)
+    return jnp.concatenate(small, axis=1)
 
 
 def split_rows(array, head_count):
@@ -54,7 +59,7 @@
     numerator = apply_weights(exponent.astype(jnp.bfloat16), value_heads)
     peak, row_total, numerator = (peak_new, row_total, numerator)
     attended = numerator / row_total[:, :, None]
-    pieces = lax.all_gather(stacked_all, "tok", axis=1, tiled=True)
+    pieces = slabs_rest(stacked_all, "tok")
     scores, tangent = score_pair(
         query_heads, query_dir_heads, pieces[0], pieces[2], head_count, score_scale
     )

time: 387 us -> 353 us (0.912)
  local copies, waits for them, and re-layouts: 109 us -> 76.3 us
    slice x2 -> x1, local copies, waits for them, and re-layouts: 39.7 us -> 7.31 us  [shards(): value_dir_heads = split_rows(pieces[3], head_count)]
    another operation x1 -> x4, local copies, waits for them, and re-layouts: 0.76 us -> 25.2 us  [split_rows(): return array.reshape(array.shape[0], head_count, HD)]
    unnamed x21 -> x23, local copies, waits for them, and re-layouts: 33.8 us -> 11.1 us
    slice x2 -> x1, local copies, waits for them, and re-layouts: 22.3 us -> 11.1 us  [shards(): value_heads = split_rows(pieces[1], head_count)]
    all_gather x0 -> x1, local copies, waits for them, and re-layouts: none -> 9.02 us  [slabs_rest(): small = lax.all_gather(block_here, axis_name=across)]
  transfers between devices with their start and end apart: 4 -> 4, of which waited for: 3 -> 3; matrix products, arithmetic and copies ran while one was open for 39% -> 33% of each run, Pallas kernels for 0% -> 0%
where the time goes in v1:
time: 353 us; the launch traced here: 352 us
  waiting for transfers between devices  220 us (62%)
  local copies, waits for them, and re-layouts  76.3 us (22%)
  matrix products  37.9 us (11%)
  between operations  13.9 us (4%)
  other arithmetic  4.07 us (1%)
    all_gather x1, waiting for transfers between devices, shards(): pieces = lax.all_gather(stacked_pair, 'tok', axis=1, tiled=True)  98.7 us
    all_gather x1, waiting for transfers between devices, slabs_rest(): small = lax.all_gather(block_here, axis_name=across)  86.7 us
    reduce_scatter x1, waiting for transfers between devices, shards(): lax.psum_scatter(partial_tan.astype(jnp.bfloat16), 'head', scatter_dimens...  34.1 us
    another operation x4, local copies, waits for them, and re-layouts, split_rows(): return array.reshape(array.shape[0], head_count, HD)  25.2 us
    slice x1, local copies, waits for them, and re-layouts, shards(): key_heads = split_rows(pieces[0], head_count)  11.8 us
    dot_general x3, matrix products, apply_weights(): jnp.einsum('htr,rhd->htd', weights, value_heads, preferred_element_type=j...  11.2 us
    slice x1, local copies, waits for them, and re-layouts, shards(): value_heads = split_rows(pieces[1], head_count)  11.1 us
    unnamed x23, local copies, waits for them, and re-layouts  11.1 us
  transfers between devices with their start and end apart: 4, of which 3 were waited for; matrix products, arithmetic and copies ran while one was open for 33% of the time, Pallas kernels for 0%

profile of v1, /device:TPU:1, one launch (start us, length us, event | category | flops | bytes accessed | tf_op | source)
XLA Modules:
  0.0 352.1 jit_solution(7211859784138011922)
XLA Ops:
  8.8 1.5 pad_maximum_fusion
  10.4 1.1 copy.38
  11.6 98.7 %all-gather.4.cloned.1.call-done = bf16[2,2048,640]{2,0,1:T(2,128)(2,1)} async-done(((bf16[2,32,640]{2,0,1:T(2,128)(2,1)}), bf16[2,2048,640]{2,0,1:T(2,128)(2,1)}) %all-gather.4.cloned.1.call-update) | async-done | bytes 5242896 | tf_op jit(solution)/shard_map/all_gather | solution.py:49
  110.3 11.8 %fusion.55 = (bf16[1,2048,640]{2,0,1:T(2,128)(2,1)}, bf16[1,2048,640]{2,0,1:T(2,128)(2,1)}) fusion(bf16[2,2048,640]{2,0,1:T(2,128)(2,1)} %all-gather.4.cloned.1.call-done), kind=kLoop, calls=%fused_computation.40 | loop fusion | bytes 10485760 | tf_op jit(solution)/shard_map/slice | solution.py:50
  122.1 9.7 %copy.61 = bf16[1,2048,640]{1,2,0:T(8,128)(2,1)S(1)} copy(bf16[1,2048,640]{2,0,1:T(2,128)(2,1)} %get-tuple-element.6) | data formatting | bytes 5242880
  131.8 11.1 %copy.41 = bf16[1,2048,640]{1,2,0:T(8,128)(2,1)} copy(bf16[1,2048,640]{2,0,1:T(2,128)(2,1)} %get-tuple-element.7) | data formatting | bytes 5242880 | tf_op jit(solution)/shard_map/slice | solution.py:51
  142.9 1.6 bitcast_reduce_fusion.1
  144.5 1.7 fusion.2
  146.3 2.7 fusion.56
  149.0 3.8 %convolution_convert_fusion.1 = bf16[256,5120]{1,0:T(8,128)(2,1)} fusion(bf16[256,640]{0,1:T(8,128)(2,1)S(1)} %bitcast.82, bf16[640,5120]{1,0:T(8,128)(2,1)S(1)} %bitcast.71), kind=kOutput, calls=%fused_computation.12 | convolution fusion | flops 1679032320 | bytes 9502720 | tf_op jit(solution)/shard_map/dot_general | solution.py:76
  153.2 86.7 %all-gather.6.cloned.1.call-done = bf16[256,32,640]{2,1,0:T(8,128)(2,1)} async-done(((bf16[4,32,640]{2,1,0:T(8,128)(2,1)}), bf16[256,32,640]{2,1,0:T(8,128)(2,1)}) %all-gather.6.cloned.1.call-update) | async-done | bytes 10485776 | tf_op jit(solution)/shard_map/all_gather | solution.py:10
  240.0 9.0 %copy.85 = bf16[64,4,32,640]{3,2,0,1:T(8,128)(2,1)} copy(bf16[64,4,32,640]{3,2,1,0:T(8,128)(2,1)} %bitcast.74) | data formatting | bytes 20971520 | tf_op jit(solution)/shard_map/all_gather | solution.py:10
  249.0 7.3 %fusion.54 = (bf16[1,64,32,640]{3,2,1,0:T(8,128)(2,1)S(1)}, bf16[1,64,32,640]{3,2,1,0:T(8,128)(2,1)}, bf16[1,64,32,640]{3,2,1,0:T(8,128)(2,1)}, bf16[1,64,32,640]{3,2,1,0:T(8,128)(2,1)}) fusion(bf16[4,64,32,640]{3,2,1,0:T(8,128)(2,1)} %bitcast.69), kind=kLoop, calls=%fused_computation.39 | loop fusion | bytes 20971520 | tf_op jit(solution)/shard_map/slice | solution.py:67
  256.3 7.0 %reshape_squeeze.22 = bf16[2048,5,128]{2,1,0:T(8,128)(2,1)} reshape(bf16[1,64,32,640]{3,2,1,0:T(8,128)(2,1)} %get-tuple-element.3) | data formatting | bytes 5242880 | tf_op jit(solution)/shard_map/reshape;squeeze | solution.py:15
  263.3 7.0 %reshape_squeeze.20 = bf16[2048,5,128]{2,1,0:T(8,128)(2,1)} reshape(bf16[1,64,32,640]{3,2,1,0:T(8,128)(2,1)} %get-tuple-element.5) | data formatting | bytes 5242880 | tf_op jit(solution)/shard_map/reshape;squeeze | solution.py:15
  270.3 7.0 %reshape_squeeze.21 = bf16[2048,5,128]{2,1,0:T(8,128)(2,1)} reshape(bf16[1,64,32,640]{3,2,1,0:T(8,128)(2,1)} %get-tuple-element.4) | data formatting | bytes 5242880 | tf_op jit(solution)/shard_map/reshape;squeeze | solution.py:15
  277.4 4.2 %reshape_squeeze.23 = bf16[2048,5,128]{2,1,0:T(8,128)(2,1)} reshape(bf16[1,64,32,640]{3,2,1,0:T(8,128)(2,1)S(1)} %get-tuple-element.2) | data formatting | bytes 5242880 | tf_op jit(solution)/shard_map/reshape;squeeze | solution.py:15
  281.6 3.9 %fusion.18 = f32[5,2048,256]{2,1,0:T(8,128)S(1)} fusion(bf16[256,5,128]{0,2,1:T(8,128)(2,1)S(1)} %bitcast.77, bf16[2048,5,128]{2,1,0:T(8,128)(2,1)} %reshape_squeeze.20), kind=kOutput, calls=%fused_computation.25 | convolution fusion | flops 671088640 | bytes 13434880 | tf_op jit(solution)/shard_map/thd,rhd->htr/dot_general | solution.py:22
  285.4 5.5 %fusion.16 = f32[5,2048,256]{2,1,0:T(8,128)} fusion(bf16[256,5,128]{0,2,1:T(8,128)(2,1)S(1)} %bitcast.80, bf16[2048,5,128]{2,1,0:T(8,128)(2,1)S(1)} %copy-done), kind=kOutput, calls=%fused_computation.23 | convolution fusion | flops 671088640 | bytes 13434880 | tf_op jit(solution)/shard_map/thd,rhd->htr/dot_general | solution.py:26
  290.9 8.2 %bitcast_reduce_fusion = (f32[5,256]{1,0:T(8,128)S(1)}, bf16[5,2048,256]{2,1,0:T(8,128)(2,1)}) fusion(f32[5,2048,256]{2,1,0:T(8,128)} %fusion.16, bf16[256,5,128]{0,2,1:T(8,128)(2,1)S(1)} %bitcast.78, bf16[2048,5,128]{2,1,0:T(8,128)(2,1)S(1)} %copy-done.2, f32[5,256]{1,0:T(8,128)S(1)} %broadcast_maximum_fusion, f32[5,2048,256]{2,1,0:T(8,128)S(1)} %fusion.18), kind=kOutput, calls=%fused_computation | convolution fusion | flops 689437440 | bytes 29173760 | tf_op jit(solution)/shard_map/thd,rhd->htr/dot_general | solution.py:27
  299.2 4.7 %fusion.8 = f32[5,256,128]{1,2,0:T(8,128)} fusion(bf16[2048,5,128]{2,1,0:T(8,128)(2,1)S(1)} %copy-done.1, bf16[5,2048,256]{2,1,0:T(8,128)(2,1)} %get-tuple-element.13), kind=kOutput, calls=%fused_computation.15 | convolution fusion | flops 671088640 | bytes 8519680 | tf_op jit(solution)/shard_map/htr,rhd->htd/dot_general | solution.py:33
  303.9 3.7 %fusion.46 = bf16[256,5,128]{0,2,1:T(8,128)(2,1)S(1)} fusion(f32[5,256,128]{1,2,0:T(8,128)} %fusion.8, f32[5,2048,256]{2,1,0:T(8,128)S(1)} %fusion.18, f32[5,256]{1,0:T(8,128)S(1)} %broadcast_maximum_fusion, bf16[2048,5,128]{2,1,0:T(8,128)(2,1)S(1)} %copy-done.3, f32[256,5,128]{0,2,1:T(8,128)} %get-tuple-element.11, f32[256,5]{0,1:T(8,128)S(1)} %bitcast.91, ...), kind=kOutput, calls=%fused_computation.33 | convolution fusion | flops 679772160 | bytes 14760960 | tf_op jit(solution)/shard_map/htr,rhd->htd/dot_general | solution.py:33
  307.6 3.8 %convolution_convert_fusion = bf16[256,5120]{1,0:T(8,128)(2,1)} fusion(bf16[256,640]{0,1:T(8,128)(2,1)S(1)} %bitcast.81, bf16[640,5120]{1,0:T(8,128)(2,1)S(1)} %bitcast.73), kind=kOutput, calls=%fused_computation.11 | convolution fusion | flops 1679032320 | bytes 9502720 | tf_op jit(solution)/shard_map/dot_general | solution.py:79
  311.5 34.1 %reduce-scatter.5.cloned.1.call-done = bf16[256,1280]{1,0:T(8,128)(2,1)} async-done(((bf16[256,5120]{1,0:T(8,128)(2,1)}), bf16[256,1280]{1,0:T(8,128)(2,1)}) %reduce-scatter.5.cloned.1.call-update) | async-done | bytes 655376 | tf_op jit(solution)/shard_map/reduce_scatter | solution.py:88
  (35 shorter events, 2.2 us)
Async XLA Ops:
  7.2 103.1 %all-gather.4.cloned.1.call-start = ((), (), s32[]{:S(2)}) async-start(), calls=%async_computation.2 | async-start | bytes 5324800 | tf_op jit(solution)/shard_map/all_gather | solution.py:49
  8.7 231.2 %all-gather.6.cloned.1.call-start = ((), (), s32[]{:S(2)}) async-start(), calls=%async_computation.5 | async-start | bytes 10649600 | tf_op jit(solution)/shard_map/all_gather | solution.py:10
  10.4 301.1 %reduce-scatter.3.cloned.1.call-start = ((), (), s32[]{:S(2)}) async-start(), calls=%async_computation.3 | async-start | bytes 3276800 | tf_op jit(solution)/shard_map/reduce_scatter | solution.py:85
  144.5 1.7 copy-start.4
  144.5 4.5 %slice-start = ((s8[6553600]{0:T(1024)(128)(4,1)}), s8[4194304]{0:T(1024)(128)(4,1)S(1)}, s32[]{:S(2)}) async-start(s8[6553600]{0:T(1024)(128)(4,1)} %bitcast.70), calls=%async_computation.6 | async-start | bytes 8388608
  146.2 2.8 slice-start.1
  149.0 4.0 %copy-start.5 = (bf16[256,640]{1,0:T(8,128)(2,1)S(1)}, bf16[256,640]{1,0:T(8,128)(2,1)}, u32[]{:S(2)}) copy-start(bf16[256,640]{1,0:T(8,128)(2,1)} %param.10) | copy-start | bytes 983044
  152.8 192.7 %reduce-scatter.5.cloned.1.call-start = ((), (), s32[]{:S(2)}) async-start(), calls=%async_computation.4 | async-start | bytes 3276800 | tf_op jit(solution)/shard_map/reduce_scatter | solution.py:88
  281.6 3.9 %copy-start = (bf16[2048,5,128]{2,1,0:T(8,128)(2,1)S(1)}, bf16[2048,5,128]{2,1,0:T(8,128)(2,1)}, u32[]{:S(2)}) copy-start(bf16[2048,5,128]{2,1,0:T(8,128)(2,1)} %reshape_squeeze.20) | copy-start | bytes 7864324
  285.4 5.5 %copy-start.2 = (bf16[2048,5,128]{2,1,0:T(8,128)(2,1)S(1)}, bf16[2048,5,128]{2,1,0:T(8,128)(2,1)}, u32[]{:S(2)}) copy-start(bf16[2048,5,128]{2,1,0:T(8,128)(2,1)} %reshape_squeeze.21) | copy-start | bytes 7864324
  290.9 8.2 %copy-start.1 = (bf16[2048,5,128]{2,1,0:T(8,128)(2,1)S(1)}, bf16[2048,5,128]{2,1,0:T(8,128)(2,1)}, u32[]{:S(2)}) copy-start(bf16[2048,5,128]{2,1,0:T(8,128)(2,1)} %reshape_squeeze.22) | copy-start | bytes 7864324
  299.1 4.7 %copy-start.3 = (bf16[2048,5,128]{2,1,0:T(8,128)(2,1)S(1)}, bf16[2048,5,128]{2,1,0:T(8,128)(2,1)}, u32[]{:S(2)}) copy-start(bf16[2048,5,128]{2,1,0:T(8,128)(2,1)} %reshape_squeeze.23) | copy-start | bytes 7864324
  299.1 8.4 %slice-start.2 = ((s8[6553600]{0:T(1024)(128)(4,1)}), s8[4194304]{0:T(1024)(128)(4,1)S(1)}, s32[]{:S(2)}) async-start(s8[6553600]{0:T(1024)(128)(4,1)} %bitcast.72), calls=%async_computation.8 | async-start | bytes 8388608
  303.9 3.7 %slice-start.3 = ((s8[6553600]{0:T(1024)(128)(4,1)}), s8[2359296]{0:T(1024)(128)(4,1)S(1)}, s32[]{:S(2)}) async-start(s8[6553600]{0:T(1024)(128)(4,1)} %bitcast.72), calls=%async_computation.9 | async-start | bytes 4718592
Sparse Core Ops, SparseCore 0:
  11.8 98.3 all-gather.3
  113.6 126.3 all-gather.5
  243.1 33.9 reduce-scatter.2
  311.6 33.9 reduce-scatter.4
